TPU v7x, 32 devices: a whole 2x2x4 slice. The times are simulated.
32 devices in a mesh: gy: 8 (over y, x, core), gz: 4 (over z).
Axes of the slice: x: 2, y: 2, z: 4, core: 2. Of those that a mesh axis runs over, the one named last changes fastest.
Arguments:
- template: float32 [16, 128, 512], P('gz', 'gy'), may hold values from -4 to 4
- target_image: float32 [16, 128, 512], P('gz', 'gy'), may hold values from -4 to 4
- departure_shifts: int32 [4, 3, 16, 128, 512], P(None, None, 'gz', 'gy'), may hold values from -2 to 1
- departure_fractions: float32 [4, 3], replicated, may hold values from 0.1 to 0.9
Outputs:
- update: float32 [3, 16, 128, 512], P(None, 'gz', 'gy')
- deformed: float32 [16, 128, 512], P('gz', 'gy')
All inputs are finite; a program needn't handle non-finite values.
Results may differ from a plain program's by a relative error of at most 0.00029.
Values sent between devices are 32-bit elements; how exact they have to be, the bound alone decides.
A program may use at most 128 MiB of HBM per device.

v0:
```python
import functools

import jax
import jax.numpy as jnp
import numpy as np
from jax import lax
from jax.experimental import pallas as pl
from jax.experimental.pallas import tpu as pltpu
from jax.sharding import PartitionSpec as P

CHEB = 8
DAMPING = 0.25
ACROSS_WEIGHT = 0.0625
ALONG_SCALE = 32.0
SHIFT = 0.25
MESH = pl.DeviceIdType.MESH
EDGE = 4
HALO = 3


def cubic_weights(fraction):
    return (
        -fraction * (fraction - 1.0) * (fraction - 2.0) / 6.0,
        (fraction + 1.0) * (fraction - 1.0) * (fraction - 2.0) / 2.0,
        -(fraction + 1.0) * fraction * (fraction - 2.0) / 2.0,
        (fraction + 1.0) * fraction * (fraction - 1.0) / 6.0,
    )


def turn_factors(count):
    low, high = SHIFT, SHIFT + 12.0
    theta, delta = (high + low) / 2.0, (high - low) / 2.0
    sigma = theta / delta
    now = 1.0 / sigma
    factors = []
    for _ in range(count - 1):
        after = 1.0 / (2.0 * sigma - now)
        factors.append((after * now, 2.0 * after / delta))
        now = after
    return theta, factors


def make_tables(rows, length_x, peers):
    length_y = rows * peers
    index = np.arange(length_x)
    angle = 2.0 * np.pi / length_x * (np.outer(index, index) % length_x)
    hartley = np.cos(angle) + np.sin(angle)
    weight = (length_y / ALONG_SCALE) ** 2
    a = DAMPING + 4.0 * ACROSS_WEIGHT * np.sin(np.pi * index / length_x) ** 2
    half = a / (2.0 * weight)
    r = 1.0 / (1.0 + half + np.sqrt(half * (half + 2.0)))
    y = np.arange(rows)[:, None]
    scale = 1.0 / (weight * (1.0 / r - r) * length_x)
    down, up, stride = [], [], 1
    while stride < rows:
        down.append(np.where(y >= stride, r ** stride, 0.0))
        up.append(np.where(y < rows - stride, r ** stride, 0.0))
        stride *= 2
    tables = [r ** (rows - 1 - y), r ** y, scale * r ** (y + 1), scale * r ** (rows - y),
              scale + 0.0 * r * y] + down + up
    m = np.arange(peers)[:, None]
    hops = r ** (rows * m) / (1.0 - r ** length_y)
    high = hartley.astype(jnp.bfloat16)
    low = (hartley - high.astype(np.float64)).astype(jnp.bfloat16)
    return high, low, np.stack(tables).astype(np.float32), hops.astype(np.float32)


def dot3(high, low, table_high, table_low):
    f = functools.partial(jnp.dot, preferred_element_type=jnp.float32)
    return f(high, table_high) + (f(low, table_high) + f(high, table_low))


def split(value):
    high = value.astype(jnp.bfloat16)
    return high, (value - high.astype(jnp.float32)).astype(jnp.bfloat16)


def choose(shift, options):
    minus2, minus1, zero, one = options
    result = jnp.where(shift == 0, zero, one)
    result = jnp.where(shift == -1, minus1, result)
    return jnp.where(shift == -2, minus2, result)


def kernel(ny, nz, fractions, *refs):
    count = 11
    sources, (update, deformed), rest = refs[:count], refs[count:count + 2], refs[count + 2:]
    held, fetch_sems, shift_sems = rest[:count], rest[count], rest[count + 1]
    step_count = held[2].shape[0]
    fetches = {}
    for i in (0, 1, 3, 4, 5, 6, 7, 8, 9, 10):
        fetches[i] = pltpu.make_async_copy(sources[i], held[i], fetch_sems.at[i])

    def fetch_shifts(step):
        return pltpu.make_async_copy(sources[2].at[step], held[2].at[step], shift_sems.at[step])

    fetches[0].start()
    for step in range(step_count):
        fetch_shifts(step).start()
    for i in (1, 7, 9, 3, 4, 5, 6, 8, 10):
        fetches[i].start()
    body(ny, nz, fractions, fetches, fetch_shifts, *held, update, deformed, *rest[count + 2:])


def body(ny, nz, fractions, fetches, fetch_shifts, template, target, shifts, hart_hi, hart_lo,
         tables, hops, pair_x, spread_x, pair_y, spread_y, update, deformed, img, ypad, yf, ysend, yrecv, zmid, zrecv, zmid_edge, zrecv_edge,
           zf, grecv, forces, ghat, msend, mrecv, coarse, left, right, dir_a, dir_b, resid, solved,
           zsum, fhi, flo, ys_send, ys_recv, zs_send, zs_recv, gs_send, gs_recv, ms_send, ms_recv,
           cs_send, cs_recv, hs_send, hs_recv):
    depth, rows, width = template.shape
    steps = shifts.shape[0]
    cz = 3 * depth
    me_y, me_z = lax.axis_index("gy"), lax.axis_index("gz")

    def at_y(offset):
        return (lax.rem(me_y + (offset + ny), ny), me_z)

    def at_z(offset):
        return (me_y, lax.rem(me_z + (offset + nz), nz))

    def copy(src, dst, send, recv, device):
        return pltpu.make_async_remote_copy(
            src_ref=src, dst_ref=dst, send_sem=send, recv_sem=recv, device_id=device,
            device_id_type=MESH)

    barrier = pltpu.get_barrier_semaphore()
    for d in range(1, ny):
        pl.semaphore_signal(barrier, inc=1, device_id=at_y(d), device_id_type=MESH)
    for d in range(1, nz):
        pl.semaphore_signal(barrier, inc=1, device_id=at_z(d), device_id_type=MESH)

    def rolled(value, by, axis):
        return pltpu.roll(value, by % value.shape[axis], axis)

    fetches[0].wait()
    for z in range(depth):
        img[z] = template[z]
    pl.semaphore_wait(barrier, ny + nz - 2)

    chunks = depth * EDGE // 8
    per = depth // chunks

    def y_copies(step, chunk):
        part = pl.ds(chunk * 8, 8)
        return [copy(ysend.at[step, side, part], yrecv.at[step, side, part],
                     ys_send.at[step, side, chunk], ys_recv.at[step, side, chunk],
                     at_y(1 - 2 * side)) for side in range(2)]

    inner = (((EDGE, rows - 2 * EDGE, 0),), zmid, zrecv, 0)
    outer = (((0, EDGE, 0), (rows - EDGE, EDGE, EDGE)), zmid_edge, zrecv_edge, 1)

    def z_copies(step, part):
        _, mid, received, which = part
        return [copy(mid.at[step, pl.ds(0 if side else depth - HALO, HALO)],
                     received.at[step, side], zs_send.at[step, side, which],
                     zs_recv.at[step, side, which], at_z(1 - 2 * side)) for side in range(2)]

    def put_edges(step, z, value):
        ypad[z, pl.ds(8, rows), :] = value
        ysend[step, 0, pl.ds(z * EDGE, EDGE), :] = value[rows - EDGE:, :]
        ysend[step, 1, pl.ds(z * EDGE, EDGE), :] = value[:EDGE, :]

    def take_edges(step, z):
        ypad[z, pl.ds(8 - EDGE, EDGE), :] = yrecv[step, 0, pl.ds(z * EDGE, EDGE), :]
        ypad[z, pl.ds(8 + rows, EDGE), :] = yrecv[step, 1, pl.ds(z * EDGE, EDGE), :]

    def advance(step, carry):
        fetch_shifts(step).wait()
        w = cubic_weights(fractions[step, 0])

        def pass_x(u, shift):
            f = (w[0] * rolled(u, 1, 1) + w[1] * u + w[2] * rolled(u, -1, 1)
                 + w[3] * rolled(u, -2, 1))
            return choose(shift, (rolled(f, 2, 1), rolled(f, 1, 1), f, rolled(f, -1, 1)))

        first, last = pl.ds(0, EDGE), pl.ds(rows - EDGE, EDGE)
        for z in range(depth):
            value = pass_x(
                jnp.concatenate([img[z, first, :], img[z, last, :]], axis=0),
                jnp.concatenate([shifts[step, 0, z, first, :], shifts[step, 0, z, last, :]],
                                axis=0))
            ypad[z, pl.ds(8, EDGE), :] = value[:EDGE, :]
            ypad[z, pl.ds(8 + rows - EDGE, EDGE), :] = value[EDGE:, :]
            ysend[step, 0, pl.ds(z * EDGE, EDGE), :] = value[EDGE:, :]
            ysend[step, 1, pl.ds(z * EDGE, EDGE), :] = value[:EDGE, :]
            if z % per == per - 1:
                for c in y_copies(step, z // per):
                    c.start()
        middle = pl.ds(EDGE, rows - 2 * EDGE)
        for z in range(depth):
            ypad[z, pl.ds(8 + EDGE, rows - 2 * EDGE), :] = pass_x(
                img[z, middle, :], shifts[step, 0, z, middle, :])
        w = cubic_weights(fractions[step, 1])

        def pass_y(part, z):
            for start, count, at in part[0]:
                f = w[0] * ypad[z, pl.ds(5 + start, count + 3), :]
                for n in range(1, 4):
                    f = f + w[n] * ypad[z, pl.ds(5 + start + n, count + 3), :]
                yf[z, pl.ds(0, count + 3), :] = f
                part[1][step, z, pl.ds(at, count), :] = choose(
                    shifts[step, 1, z, pl.ds(start, count), :],
                    [yf[z, pl.ds(o, count), :] for o in range(4)])

        for z in range(depth):
            pass_y(inner, z)
        for c in z_copies(step, inner):
            c.start()
        for z in range(depth):
            if z % per == 0:
                for c in y_copies(step, z // per):
                    c.wait_recv()
            take_edges(step, z)
            pass_y(outer, z)
        for c in z_copies(step, outer):
            c.start()
        w_z = cubic_weights(fractions[step, 2])

        def pass_z(part):
            pieces, mid, received, _ = part
            for c in z_copies(step, part):
                c.wait_recv()
            size = sum(count for _, count, _ in pieces)

            def layer(k):
                if k < HALO:
                    return received[step, 0, k]
                if k < HALO + depth:
                    return mid[step, k - HALO]
                return received[step, 1, k - HALO - depth]

            for k in range(depth + 3):
                zf[k, pl.ds(0, size), :] = (w_z[0] * layer(k) + w_z[1] * layer(k + 1)
                                            + w_z[2] * layer(k + 2) + w_z[3] * layer(k + 3))
            for z in range(depth):
                for start, count, at in pieces:
                    img[z, pl.ds(start, count), :] = choose(
                        shifts[step, 2, z, pl.ds(start, count), :],
                        [zf[z + o, pl.ds(at, count), :] for o in range(4)])

        pass_z(inner)
        pass_z(outer)
        for chunk in range(chunks):
            for c in y_copies(step, chunk):
                c.wait_send()
        for part in (inner, outer):
            for c in z_copies(step, part):
                c.wait_send()
        return carry

    lax.fori_loop(0, steps, advance, 0)

    for z in range(depth):
        put_edges(steps, z, img[z])
    copies = [c for chunk in range(chunks) for c in y_copies(steps, chunk)] + [
        copy(img.at[depth - 1], grecv.at[0], gs_send.at[0], gs_recv.at[0], at_z(1)),
        copy(img.at[0], grecv.at[1], gs_send.at[1], gs_recv.at[1], at_z(-1)),
    ]
    for c in copies:
        c.start()
    fetches[1].wait()
    for z in range(depth):
        u = img[z]
        deformed[z] = u
        forces[pl.ds(z * rows, rows), :] = (
            (u - target[z]) * ((rolled(u, -1, 1) - rolled(u, 1, 1)) * 0.5))
    for c in copies:
        c.wait()
    for z in range(depth):
        take_edges(steps, z)
        mismatch = img[z] - target[z]
        grad = (ypad[z, pl.ds(9, rows), :] - ypad[z, pl.ds(7, rows), :]) * 0.5
        forces[pl.ds((depth + z) * rows, rows), :] = mismatch * grad
        above = img[z + 1] if z + 1 < depth else grecv[1]
        below = img[z - 1] if z > 0 else grecv[0]
        forces[pl.ds((2 * depth + z) * rows, rows), :] = mismatch * ((above - below) * 0.5)

    dc, rc, wc = depth // 2, rows // 2, width // 2
    for c in range(3):
        for z in range(dc):
            base = (c * depth + 2 * z) * rows
            zsum[pl.ds((c * dc + z) * rows, rows), :] = (
                forces[pl.ds(base, rows), :] + forces[pl.ds(base + rows, rows), :])
    fetches[7].wait()
    fetches[9].wait()
    high, low = split(zsum[...])
    f32dot = functools.partial(jnp.dot, preferred_element_type=jnp.float32)
    summed = f32dot(high, pair_x[...]) + f32dot(low, pair_x[...])
    high, low = split(summed)
    coarse[0] = f32dot(pair_y[...], high) + f32dot(pair_y[...], low)
    gathers = [copy(coarse.at[0], coarse.at[d], cs_send.at[d - 1], cs_recv.at[d - 1], at_z(-d))
               for d in range(1, nz)]
    for c in gathers:
        c.start()
    sides = [[copy(coarse.at[d], left.at[d], hs_send.at[0, d], hs_recv.at[0, d], at_y(1)),
              copy(coarse.at[d], right.at[d], hs_send.at[1, d], hs_recv.at[1, d], at_y(-1))]
             for d in range(nz)]
    for c in sides[0]:
        c.start()

    for i in (3, 4, 5):
        fetches[i].wait()
    high, low = split(forces[...])
    ghat[...] = dot3(high, low, hart_hi[...], hart_lo[...])
    for k in range(cz):
        g = ghat[pl.ds(k * rows, rows), :]
        msend[pl.ds(k, 1), :] = jnp.sum(g * tables[0], axis=0, keepdims=True)
        msend[pl.ds(cz + k, 1), :] = jnp.sum(g * tables[1], axis=0, keepdims=True)
    moments = [copy(msend, mrecv.at[d - 1], ms_send.at[d - 1], ms_recv.at[d - 1], at_y(d))
               for d in range(1, ny)]
    for c in moments:
        c.start()
    for d in sorted(range(1, nz), key=lambda d: min(d, nz - d)):
        gathers[d - 1].wait()
        for c in sides[d]:
            c.start()
    for c in moments:
        c.wait()
    fetches[6].wait()
    from_left = hops[pl.ds(ny - 1, 1), :] * msend[pl.ds(0, cz), :]
    from_right = hops[pl.ds(ny - 1, 1), :] * msend[pl.ds(cz, cz), :]
    for m in range(1, ny):
        from_left = from_left + hops[pl.ds(m - 1, 1), :] * mrecv[m - 1, pl.ds(0, cz), :]
        from_right = from_right + hops[pl.ds(m - 1, 1), :] * mrecv[ny - m - 1, pl.ds(cz, cz), :]
    levels = (tables.shape[0] - 5) // 2
    for k in range(cz):
        g = ghat[pl.ds(k * rows, rows), :]
        down, up = g, g
        for level in range(levels):
            down = down + tables[5 + level] * rolled(down, 1 << level, 0)
            up = up + tables[5 + levels + level] * rolled(up, -(1 << level), 0)
        s = (tables[4] * (down + (up - g)) + tables[2] * from_left[k:k + 1, :]
             + tables[3] * from_right[k:k + 1, :])
        high, low = split(s)
        fhi[pl.ds(k * rows, rows), :] = high
        flo[pl.ds(k * rows, rows), :] = low
    ghat[...] = dot3(fhi[...], flo[...], hart_hi[...], hart_lo[...])

    for pair in sides:
        for c in pair:
            c.wait()
    theta, factors = turn_factors(CHEB)
    for d in range(nz):
        for c in range(3):
            for zl in range(dc):
                part = pl.ds((c * dc + zl) * rc, rc)
                for i, source in enumerate((left, coarse, right)):
                    value = source[d, part, :]
                    resid[d * dc + zl, c, pl.ds(i * rc, rc), :] = value
                    dir_a[d * dc + zl, c, pl.ds(i * rc, rc), :] = value * (1.0 / theta)
    total = nz * dc
    for c in range(3):
        for zl in range(dc):
            solved[pl.ds((c * dc + zl) * rc, rc), :] = dir_a[zl, c, pl.ds(rc, rc), :]
    now, later = dir_a, dir_b
    for turn, (keep, add) in enumerate(factors):
        reach = len(factors) - 1 - turn
        count = min(total, dc + 2 * reach)

        def relax(i, carry, now=now, later=later, reach=reach, keep=keep, add=add):
            z = lax.rem(i + (total * CHEB - reach), total)
            above, below = lax.rem(z + 1, total), lax.rem(z + (total - 1), total)
            for c in range(3):
                v = now[z, c]
                beside = now[above, c] + now[below, c]
                beside = beside + rolled(v, -1, 0) + rolled(v, 1, 0)
                beside = beside + rolled(v, -1, 1) + rolled(v, 1, 1)
                res = resid[z, c] - ((SHIFT + 6.0) * v - beside)
                resid[z, c] = res
                later[z, c] = keep * v + add * res
            return carry

        lax.fori_loop(0, count, relax, 0)
        for c in range(3):
            for zl in range(dc):
                part = pl.ds((c * dc + zl) * rc, rc)
                solved[part, :] = solved[part, :] + later[zl, c, pl.ds(rc, rc), :]
        now, later = later, now

    fetches[8].wait()
    fetches[10].wait()
    high, low = split(solved[...])
    tall = f32dot(spread_y[...], high) + f32dot(spread_y[...], low)
    high, low = split(tall)
    zsum[...] = f32dot(high, spread_x[...]) + f32dot(low, spread_x[...])
    for c in range(3):
        for z in range(depth):
            fine = zsum[pl.ds((c * dc + z // 2) * rows, rows), :]
            update[c, z] = -(ghat[pl.ds((c * depth + z) * rows, rows), :] + fine)


def on_device(template, target, shifts, fractions, *, ny, nz):
    depth, rows, width = template.shape
    steps = shifts.shape[0]
    dc, rc, wc = depth // 2, rows // 2, width // 2
    cz = 3 * depth
    hart_hi, hart_lo, tables, hops = make_tables(rows, width, ny)
    pair_x = np.kron(np.eye(wc), np.full((2, 1), 0.125)).astype(jnp.bfloat16)
    spread_x = np.kron(np.eye(wc), np.ones((1, 2))).astype(jnp.bfloat16)
    pair_y = np.kron(np.eye(3 * dc * rc), np.ones((1, 2))).astype(jnp.bfloat16)
    spread_y = np.ascontiguousarray(pair_y.T)
    f32, bf16 = jnp.float32, jnp.bfloat16
    vmem, dma = pltpu.VMEM, pltpu.SemaphoreType.DMA
    total = nz * dc
    scratch = [
        vmem((depth, rows, width), f32),
        vmem((depth, rows + 16, width), f32),
        vmem((depth, rows + 8, width), f32),
        vmem((steps + 1, 2, depth * EDGE, width), f32),
        vmem((steps + 1, 2, depth * EDGE, width), f32),
        vmem((steps, depth, rows - 2 * EDGE, width), f32),
        vmem((steps, 2, HALO, rows - 2 * EDGE, width), f32),
        vmem((steps, depth, 2 * EDGE, width), f32),
        vmem((steps, 2, HALO, 2 * EDGE, width), f32),
        vmem((depth + 3, rows, width), f32),
        vmem((2, rows, width), f32),
        vmem((cz * rows, width), f32),
        vmem((cz * rows, width), f32),
        vmem((2 * cz, width), f32),
        vmem((ny - 1, 2 * cz, width), f32),
        vmem((nz, 3 * dc * rc, wc), f32),
        vmem((nz, 3 * dc * rc, wc), f32),
        vmem((nz, 3 * dc * rc, wc), f32),
        vmem((total, 3, 3 * rc, wc), f32),
        vmem((total, 3, 3 * rc, wc), f32),
        vmem((total, 3, 3 * rc, wc), f32),
        vmem((3 * dc * rc, wc), f32),
        vmem((3 * dc * rows, width), f32),
        vmem((cz * rows, width), bf16),
        vmem((cz * rows, width), bf16),
        dma((steps + 1, 2, depth * EDGE // 8)), dma((steps + 1, 2, depth * EDGE // 8)),
        dma((steps, 2, 2)), dma((steps, 2, 2)),
        dma((2,)), dma((2,)),
        dma((ny - 1,)), dma((ny - 1,)),
        dma((nz - 1,)), dma((nz - 1,)),
        dma((2, nz)), dma((2, nz)),
    ]
    spec = pl.BlockSpec(memory_space=pltpu.VMEM)
    smem = pl.BlockSpec(memory_space=pltpu.SMEM)
    hbm = pl.BlockSpec(memory_space=pltpu.HBM)
    operands = [template, target, shifts, jnp.asarray(hart_hi), jnp.asarray(hart_lo),
                jnp.asarray(tables), jnp.asarray(hops), jnp.asarray(pair_x),
                jnp.asarray(spread_x), jnp.asarray(pair_y), jnp.asarray(spread_y)]
    held = [vmem(x.shape, x.dtype) for x in operands]
    scratch = held + [dma((len(operands),)), dma((steps,))] + scratch
    return tuple(pl.pallas_call(
        functools.partial(kernel, ny, nz),
        out_shape=(jax.ShapeDtypeStruct((3, depth, rows, width), f32),
                   jax.ShapeDtypeStruct((depth, rows, width), f32)),
        in_specs=[smem] + [hbm] * len(operands),
        out_specs=(spec, spec),
        scratch_shapes=scratch,
        compiler_params=pltpu.CompilerParams(
            collective_id=0, has_side_effects=True),
    )(fractions, *operands))


def solution(mesh):
    return jax.shard_map(
        functools.partial(on_device, ny=mesh.shape["gy"], nz=mesh.shape["gz"]),
        mesh=mesh,
        in_specs=(P("gz", "gy", None), P("gz", "gy", None), P(None, None, "gz", "gy", None), P()),
        out_specs=(P(None, "gz", "gy", None), P("gz", "gy", None)),
        check_vma=False,
    )
```

profile of v0, /device:TPU:1, one launch (start us, length us, event | category | flops | bytes accessed | tf_op | source)
XLA Modules:
  0.0 62.0 jit_solution(3195757018828008699)
XLA Ops:
  0.6 58.1 %shard_map.131 = (f32[3,4,16,512]{3,2,1,0:T(8,128)}, f32[4,16,512]{2,1,0:T(8,128)}) custom-call(f32[4,3]{1,0:T(4,128)} %fractions.1, f32[4,16,512]{2,1,0:T(8,128)} %refs_0_.1, f32[4,16,512]{2,1,0:T(8,128)} %refs_1_.1, s32[4,3,4,16,512]{4,3,2,1,0:T(8,128)} %refs_2_.1, bf16[512,512]{1,0:T(8,128)(2,1)} %constant.16.clone.refs_3_, ...), custom_call_target="tpu_custom_call" | custom-call | tf_op jit(solution)/shard_map/pallas_call | solution.py:446
  58.7 1.8 %copy.16 = f32[3,4,16,512]{3,2,1,0:T(8,128)} copy(f32[3,4,16,512]{3,2,1,0:T(8,128)} %get-tuple-element.4) | data formatting | bytes 786432
  60.5 1.6 %copy.17 = f32[4,16,512]{2,1,0:T(8,128)} copy(f32[4,16,512]{2,1,0:T(8,128)} %get-tuple-element.5) | data formatting | bytes 262144
where the time goes:
time: 62.2 us; the launch traced here: 62 us
  Pallas kernels  58.1 us (93%)
  local copies, waits for them, and re-layouts  3.33 us (5%)
  between operations  0.64 us (1%)
    pallas_call x1, Pallas kernels, on_device(): pl.pallas_call(functools.partial(kernel, ny, nz), out_shape=(jax.ShapeDty...  58.1 us
    unnamed x2, local copies, waits for them, and re-layouts  3.33 us

commit v1 on v0

--- a/solution.py
+++ b/solution.py
@@ -445,8 +445,7 @@
     scratch = held + [dma((len(operands),)), dma((steps,))] + scratch
     return tuple(pl.pallas_call(
         functools.partial(kernel, ny, nz),
-        out_shape=(jax.ShapeDtypeStruct((3, depth, rows, width), f32),
-                   jax.ShapeDtypeStruct((depth, rows, width), f32)),
+        out_shape=(vmem((3, depth, rows, width), f32), vmem((depth, rows, width), f32)),
         in_specs=[smem] + [hbm] * len(operands),
         out_specs=(spec, spec),
         scratch_shapes=scratch,

time: 62.2 us -> 59.5 us (0.957)
  local copies, waits for them, and re-layouts: 3.33 us -> 1.4 us
  Pallas kernels: 58.1 us -> 57.3 us
    unnamed x2, local copies, waits for them, and re-layouts: 3.33 us -> 1.4 us
    pallas_call x1, Pallas kernels: 58.1 us -> 57.3 us  [on_device(): pl.pallas_call(functools.partial(kernel, ny, nz), out_shape=(vmem((3, dep...]
where the time goes in v1:
time: 59.5 us; the launch traced here: 59.4 us
  Pallas kernels  57.3 us (96%)
  local copies, waits for them, and re-layouts  1.4 us (2%)
  between operations  0.64 us (1%)
    pallas_call x1, Pallas kernels, on_device(): pl.pallas_call(functools.partial(kernel, ny, nz), out_shape=(vmem((3, dep...  57.3 us
    unnamed x2, local copies, waits for them, and re-layouts  1.4 us

profile of v1, /device:TPU:1, one launch (start us, length us, event | category | flops | bytes accessed | tf_op | source)
XLA Modules:
  0.0 59.4 jit_solution(4710824451996544009)
XLA Ops:
  0.6 57.3 %shard_map.131 = (f32[3,4,16,512]{3,2,1,0:T(8,128)S(1)}, f32[4,16,512]{2,1,0:T(8,128)S(1)}) custom-call(f32[4,3]{1,0:T(4,128)} %fractions.1, f32[4,16,512]{2,1,0:T(8,128)} %refs_0_.1, f32[4,16,512]{2,1,0:T(8,128)} %refs_1_.1, s32[4,3,4,16,512]{4,3,2,1,0:T(8,128)} %refs_2_.1, bf16[512,512]{1,0:T(8,128)(2,1)} %constant.16.clone.refs_3_, ...), custom_call_target="tpu_custom_call" | custom-call | tf_op jit(solution)/shard_map/pallas_call | solution.py:446
  58.0 0.7 %copy.16 = f32[3,4,16,512]{3,2,1,0:T(8,128)} copy(f32[3,4,16,512]{3,2,1,0:T(8,128)S(1)} %get-tuple-element.2) | data formatting | bytes 786432
  58.7 0.7 %copy.17 = f32[4,16,512]{2,1,0:T(8,128)} copy(f32[4,16,512]{2,1,0:T(8,128)S(1)} %get-tuple-element.3) | data formatting | bytes 262144

commit v2 on v1

--- a/solution.py
+++ b/solution.py
@@ -65,6 +65,46 @@
     return high, low, np.stack(tables).astype(np.float32), hops.astype(np.float32)
 
 
+def cas(length):
+    index = np.arange(length)
+    angle = 2.0 * np.pi / length * (np.outer(index, index) % length)
+    return np.cos(angle) + np.sin(angle)
+
+
+def in_two(table):
+    high = table.astype(jnp.bfloat16)
+    return high, (table - high.astype(np.float64)).astype(jnp.bfloat16)
+
+
+def far_layers(total):
+    return min(total // 2, CHEB - 1) + 1
+
+
+def make_coarse(width, total, length_y):
+    half = width // 2
+    pair = np.kron(np.eye(half), np.full((2, 1), 0.125))
+    fold = in_two(pair @ cas(half))
+    spread = in_two(cas(half) @ np.kron(np.eye(half), np.ones((1, 2))) / half)
+    x, y, z = [2.0 * np.cos(2.0 * np.pi * np.arange(n) / n) for n in (half, length_y, total)]
+    symbol = SHIFT + 6.0 - (z[:, None, None] + y[None, :, None] + x[None, None, :])
+    theta, factors = turn_factors(CHEB)
+    residual = np.ones_like(symbol)
+    direction = residual / theta
+    gain = direction
+    for keep, add in factors:
+        residual = residual - symbol * direction
+        direction = keep * direction + add * residual
+        gain = gain + direction
+    taps = []
+    for dz in range(far_layers(total)):
+        in_z = np.cos(2.0 * np.pi * dz * np.arange(total) / total) / total
+        plane = np.tensordot(in_z, gain, 1)
+        for dy in range(CHEB - dz):
+            in_y = np.cos(2.0 * np.pi * dy * np.arange(length_y) / length_y) / length_y
+            taps.append(in_y @ plane)
+    return fold + spread + (np.stack(taps).astype(np.float32),)
+
+
 def dot3(high, low, table_high, table_low):
     f = functools.partial(jnp.dot, preferred_element_type=jnp.float32)
     return f(high, table_high) + (f(low, table_high) + f(high, table_low))
@@ -83,12 +123,12 @@
 
 
 def kernel(ny, nz, fractions, *refs):
-    count = 11
+    count = 14
     sources, (update, deformed), rest = refs[:count], refs[count:count + 2], refs[count + 2:]
     held, fetch_sems, shift_sems = rest[:count], rest[count], rest[count + 1]
     step_count = held[2].shape[0]
     fetches = {}
-    for i in (0, 1, 3, 4, 5, 6, 7, 8, 9, 10):
+    for i in (0, 1, *range(3, count)):
         fetches[i] = pltpu.make_async_copy(sources[i], held[i], fetch_sems.at[i])
 
     def fetch_shifts(step):
@@ -97,14 +137,15 @@
     fetches[0].start()
     for step in range(step_count):
         fetch_shifts(step).start()
-    for i in (1, 7, 9, 3, 4, 5, 6, 8, 10):
+    for i in (1, 7, 8, 11, 3, 4, 5, 6, 13, 9, 10, 12):
         fetches[i].start()
     body(ny, nz, fractions, fetches, fetch_shifts, *held, update, deformed, *rest[count + 2:])
 
 
 def body(ny, nz, fractions, fetches, fetch_shifts, template, target, shifts, hart_hi, hart_lo,
-         tables, hops, pair_x, spread_x, pair_y, spread_y, update, deformed, img, ypad, yf, ysend, yrecv, zmid, zrecv, zmid_edge, zrecv_edge,
-           zf, grecv, forces, ghat, msend, mrecv, coarse, left, right, dir_a, dir_b, resid, solved,
+         tables, hops, fold_hi, fold_lo, spread_hi, spread_lo, pair_y, spread_y, taps,
+         update, deformed, img, ypad, yf, ysend, yrecv, zmid, zrecv, zmid_edge, zrecv_edge,
+           zf, grecv, forces, ghat, msend, mrecv, coarse, parts, arrived, mixed,
            zsum, fhi, flo, ys_send, ys_recv, zs_send, zs_recv, gs_send, gs_recv, ms_send, ms_recv,
            cs_send, cs_recv, hs_send, hs_recv):
     depth, rows, width = template.shape
@@ -132,6 +173,7 @@
     def rolled(value, by, axis):
         return pltpu.roll(value, by % value.shape[axis], axis)
 
+    mixed[...] = jnp.zeros_like(mixed)
     fetches[0].wait()
     for z in range(depth):
         img[z] = template[z]
@@ -281,21 +323,21 @@
             base = (c * depth + 2 * z) * rows
             zsum[pl.ds((c * dc + z) * rows, rows), :] = (
                 forces[pl.ds(base, rows), :] + forces[pl.ds(base + rows, rows), :])
-    fetches[7].wait()
-    fetches[9].wait()
+    for i in (7, 8, 11):
+        fetches[i].wait()
+    f32dot = functools.partial(jnp.dot, preferred_element_type=jnp.float32)
     high, low = split(zsum[...])
-    f32dot = functools.partial(jnp.dot, preferred_element_type=jnp.float32)
-    summed = f32dot(high, pair_x[...]) + f32dot(low, pair_x[...])
-    high, low = split(summed)
+    high, low = split(dot3(high, low, fold_hi[...], fold_lo[...]))
     coarse[0] = f32dot(pair_y[...], high) + f32dot(pair_y[...], low)
-    gathers = [copy(coarse.at[0], coarse.at[d], cs_send.at[d - 1], cs_recv.at[d - 1], at_z(-d))
-               for d in range(1, nz)]
+    gathers = []
+    for k in range(nz - 1):
+        away = jnp.where(me_z < nz // 2, nz - 1 - k, k)
+        away = away + jnp.where(me_z < nz // 2, -(away <= me_z).astype(jnp.int32),
+                                (away >= me_z).astype(jnp.int32))
+        slot = lax.rem(me_z - away + nz, nz)
+        gathers.append(copy(coarse.at[0], coarse.at[slot], cs_send.at[slot - 1],
+                            cs_recv.at[slot - 1], (me_y, away)))
     for c in gathers:
-        c.start()
-    sides = [[copy(coarse.at[d], left.at[d], hs_send.at[0, d], hs_recv.at[0, d], at_y(1)),
-              copy(coarse.at[d], right.at[d], hs_send.at[1, d], hs_recv.at[1, d], at_y(-1))]
-             for d in range(nz)]
-    for c in sides[0]:
         c.start()
 
     for i in (3, 4, 5):
@@ -310,10 +352,49 @@
                for d in range(1, ny)]
     for c in moments:
         c.start()
-    for d in sorted(range(1, nz), key=lambda d: min(d, nz - d)):
-        gathers[d - 1].wait()
-        for c in sides[d]:
-            c.start()
+    fetches[13].wait()
+    for d in range(1, nz):
+        copy(coarse.at[0], coarse.at[d], cs_send.at[d - 1], cs_recv.at[d - 1], at_z(-d)).wait()
+    total, far = nz * dc, far_layers(nz * dc)
+    lanes = min(wc, 128)
+    for c in range(3):
+        for h in range(wc // lanes):
+            across = pl.ds(h * lanes, lanes)
+
+            def level(z, c=c, across=across):
+                return coarse[z % total // dc, pl.ds((c * dc + z % dc) * rc, rc), across]
+
+            for a in range(dc):
+                for dz in range(far):
+                    value = level(a + dz)
+                    if 0 < dz and 2 * dz != total:
+                        value = value + level(a + total - dz)
+                    mixed[h, a * far + dz, pl.ds(rc, rc), :] = value
+            for a in range(dc):
+                sums = [None] * 3
+
+                def add(side, value):
+                    sums[side] = value if sums[side] is None else sums[side] + value
+
+                row = 0
+                for dz in range(far):
+                    for dy in range(CHEB - dz):
+                        tap = taps[pl.ds(row, 1), across]
+                        row += 1
+                        at = [mixed[h, a * far + dz, pl.ds(o, rc), :]
+                              for o in (dy, rc - dy, rc + dy, 2 * rc - dy)]
+                        if dy == 0:
+                            add(0, tap * at[1])
+                        else:
+                            add(0, tap * (at[1] + at[2]))
+                            add(1, tap * at[0])
+                            add(2, tap * at[3])
+                for side in range(3):
+                    parts[side, pl.ds((c * dc + a) * rc, rc), across] = sums[side]
+    sides = [copy(parts.at[1], arrived.at[0], hs_send.at[0], hs_recv.at[0], at_y(-1)),
+             copy(parts.at[2], arrived.at[1], hs_send.at[1], hs_recv.at[1], at_y(1))]
+    for c in sides:
+        c.start()
     for c in moments:
         c.wait()
     fetches[6].wait()
@@ -336,53 +417,14 @@
         flo[pl.ds(k * rows, rows), :] = low
     ghat[...] = dot3(fhi[...], flo[...], hart_hi[...], hart_lo[...])
 
-    for pair in sides:
-        for c in pair:
-            c.wait()
-    theta, factors = turn_factors(CHEB)
-    for d in range(nz):
-        for c in range(3):
-            for zl in range(dc):
-                part = pl.ds((c * dc + zl) * rc, rc)
-                for i, source in enumerate((left, coarse, right)):
-                    value = source[d, part, :]
-                    resid[d * dc + zl, c, pl.ds(i * rc, rc), :] = value
-                    dir_a[d * dc + zl, c, pl.ds(i * rc, rc), :] = value * (1.0 / theta)
-    total = nz * dc
-    for c in range(3):
-        for zl in range(dc):
-            solved[pl.ds((c * dc + zl) * rc, rc), :] = dir_a[zl, c, pl.ds(rc, rc), :]
-    now, later = dir_a, dir_b
-    for turn, (keep, add) in enumerate(factors):
-        reach = len(factors) - 1 - turn
-        count = min(total, dc + 2 * reach)
-
-        def relax(i, carry, now=now, later=later, reach=reach, keep=keep, add=add):
-            z = lax.rem(i + (total * CHEB - reach), total)
-            above, below = lax.rem(z + 1, total), lax.rem(z + (total - 1), total)
-            for c in range(3):
-                v = now[z, c]
-                beside = now[above, c] + now[below, c]
-                beside = beside + rolled(v, -1, 0) + rolled(v, 1, 0)
-                beside = beside + rolled(v, -1, 1) + rolled(v, 1, 1)
-                res = resid[z, c] - ((SHIFT + 6.0) * v - beside)
-                resid[z, c] = res
-                later[z, c] = keep * v + add * res
-            return carry
-
-        lax.fori_loop(0, count, relax, 0)
-        for c in range(3):
-            for zl in range(dc):
-                part = pl.ds((c * dc + zl) * rc, rc)
-                solved[part, :] = solved[part, :] + later[zl, c, pl.ds(rc, rc), :]
-        now, later = later, now
-
-    fetches[8].wait()
-    fetches[10].wait()
-    high, low = split(solved[...])
+    for i in (9, 10, 12):
+        fetches[i].wait()
+    for c in sides:
+        c.wait()
+    high, low = split(parts[0] + (arrived[0] + arrived[1]))
     tall = f32dot(spread_y[...], high) + f32dot(spread_y[...], low)
     high, low = split(tall)
-    zsum[...] = f32dot(high, spread_x[...]) + f32dot(low, spread_x[...])
+    zsum[...] = dot3(high, low, spread_hi[...], spread_lo[...])
     for c in range(3):
         for z in range(depth):
             fine = zsum[pl.ds((c * dc + z // 2) * rows, rows), :]
@@ -395,13 +437,11 @@
     dc, rc, wc = depth // 2, rows // 2, width // 2
     cz = 3 * depth
     hart_hi, hart_lo, tables, hops = make_tables(rows, width, ny)
-    pair_x = np.kron(np.eye(wc), np.full((2, 1), 0.125)).astype(jnp.bfloat16)
-    spread_x = np.kron(np.eye(wc), np.ones((1, 2))).astype(jnp.bfloat16)
+    fold_hi, fold_lo, spread_hi, spread_lo, taps = make_coarse(width, nz * dc, ny * rc)
     pair_y = np.kron(np.eye(3 * dc * rc), np.ones((1, 2))).astype(jnp.bfloat16)
     spread_y = np.ascontiguousarray(pair_y.T)
     f32, bf16 = jnp.float32, jnp.bfloat16
     vmem, dma = pltpu.VMEM, pltpu.SemaphoreType.DMA
-    total = nz * dc
     scratch = [
         vmem((depth, rows, width), f32),
         vmem((depth, rows + 16, width), f32),
@@ -419,12 +459,9 @@
         vmem((2 * cz, width), f32),
         vmem((ny - 1, 2 * cz, width), f32),
         vmem((nz, 3 * dc * rc, wc), f32),
-        vmem((nz, 3 * dc * rc, wc), f32),
-        vmem((nz, 3 * dc * rc, wc), f32),
-        vmem((total, 3, 3 * rc, wc), f32),
-        vmem((total, 3, 3 * rc, wc), f32),
-        vmem((total, 3, 3 * rc, wc), f32),
-        vmem((3 * dc * rc, wc), f32),
+        vmem((3, 3 * dc * rc, wc), f32),
+        vmem((2, 3 * dc * rc, wc), f32),
+        vmem((-(-wc // 128), dc * far_layers(nz * dc), 3 * rc, min(wc, 128)), f32),
         vmem((3 * dc * rows, width), f32),
         vmem((cz * rows, width), bf16),
         vmem((cz * rows, width), bf16),
@@ -433,14 +470,14 @@
         dma((2,)), dma((2,)),
         dma((ny - 1,)), dma((ny - 1,)),
         dma((nz - 1,)), dma((nz - 1,)),
-        dma((2, nz)), dma((2, nz)),
+        dma((2,)), dma((2,)),
     ]
     spec = pl.BlockSpec(memory_space=pltpu.VMEM)
     smem = pl.BlockSpec(memory_space=pltpu.SMEM)
     hbm = pl.BlockSpec(memory_space=pltpu.HBM)
     operands = [template, target, shifts, jnp.asarray(hart_hi), jnp.asarray(hart_lo),
-                jnp.asarray(tables), jnp.asarray(hops), jnp.asarray(pair_x),
-                jnp.asarray(spread_x), jnp.asarray(pair_y), jnp.asarray(spread_y)]
+                *map(jnp.asarray, (tables, hops, fold_hi, fold_lo, spread_hi, spread_lo, pair_y,
+                                   spread_y, taps))]
     held = [vmem(x.shape, x.dtype) for x in operands]
     scratch = held + [dma((len(operands),)), dma((steps,))] + scratch
     return tuple(pl.pallas_call(

time: 59.5 us -> 52.7 us (0.89)
  Pallas kernels: 57.3 us -> 50.5 us
    pallas_call x1, Pallas kernels: 57.3 us -> 50.5 us  [on_device(): pl.pallas_call(functools.partial(kernel, ny, nz), out_shape=(vmem((3, dep...]
where the time goes in v2:
time: 52.7 us; the launch traced here: 52.6 us
  Pallas kernels  50.5 us (96%)
  local copies, waits for them, and re-layouts  1.4 us (3%)
  between operations  0.64 us (1%)
    pallas_call x1, Pallas kernels, on_device(): pl.pallas_call(functools.partial(kernel, ny, nz), out_shape=(vmem((3, dep...  50.5 us
    unnamed x2, local copies, waits for them, and re-layouts  1.4 us

profile of v2, /device:TPU:1, one launch (start us, length us, event | category | flops | bytes accessed | tf_op | source)
XLA Modules:
  0.0 52.6 jit_solution(11799905028431488313)
XLA Ops:
  0.6 50.5 %shard_map.158 = (f32[3,4,16,512]{3,2,1,0:T(8,128)S(1)}, f32[4,16,512]{2,1,0:T(8,128)S(1)}) custom-call(f32[4,3]{1,0:T(4,128)} %fractions.1, f32[4,16,512]{2,1,0:T(8,128)} %refs_0_.1, f32[4,16,512]{2,1,0:T(8,128)} %refs_1_.1, s32[4,3,4,16,512]{4,3,2,1,0:T(8,128)} %refs_2_.1, bf16[512,512]{1,0:T(8,128)(2,1)} %constant.22.clone.refs_3_, ...), custom_call_target="tpu_custom_call" | custom-call | tf_op jit(solution)/shard_map/pallas_call | solution.py:483
  51.2 0.7 %copy.19 = f32[3,4,16,512]{3,2,1,0:T(8,128)} copy(f32[3,4,16,512]{3,2,1,0:T(8,128)S(1)} %get-tuple-element.2) | data formatting | bytes 786432
  51.9 0.7 %copy.20 = f32[4,16,512]{2,1,0:T(8,128)} copy(f32[4,16,512]{2,1,0:T(8,128)S(1)} %get-tuple-element.3) | data formatting | bytes 262144

commit v3 on v2

--- a/solution.py
+++ b/solution.py
@@ -139,14 +139,14 @@
         fetch_shifts(step).start()
     for i in (1, 7, 8, 11, 3, 4, 5, 6, 13, 9, 10, 12):
         fetches[i].start()
-    body(ny, nz, fractions, fetches, fetch_shifts, *held, update, deformed, *rest[count + 2:])
-
-
-def body(ny, nz, fractions, fetches, fetch_shifts, template, target, shifts, hart_hi, hart_lo,
+    body(ny, nz, fractions, fetches, fetch_shifts, sources[2], *held, update, deformed, *rest[count + 2:])
+
+
+def body(ny, nz, fractions, fetches, fetch_shifts, all_shifts, template, target, shifts, hart_hi, hart_lo,
          tables, hops, fold_hi, fold_lo, spread_hi, spread_lo, pair_y, spread_y, taps,
          update, deformed, img, ypad, yf, ysend, yrecv, zmid, zrecv, zmid_edge, zrecv_edge,
-           zf, grecv, forces, ghat, msend, mrecv, coarse, parts, arrived, mixed,
-           zsum, fhi, flo, ys_send, ys_recv, zs_send, zs_recv, gs_send, gs_recv, ms_send, ms_recv,
+           zf, beyond, zshift, yshift_send, yshift, rim, rim_rows, rim_f, forces, ghat, msend, mrecv, coarse, parts, arrived, mixed,
+           zsum, fhi, flo, ys_send, ys_recv, zs_send, zs_recv, rs_send, rs_recv, zh_send, zh_recv, yh_send, yh_recv, ms_send, ms_recv,
            cs_send, cs_recv, hs_send, hs_recv):
     depth, rows, width = template.shape
     steps = shifts.shape[0]
@@ -173,12 +173,6 @@
     def rolled(value, by, axis):
         return pltpu.roll(value, by % value.shape[axis], axis)
 
-    mixed[...] = jnp.zeros_like(mixed)
-    fetches[0].wait()
-    for z in range(depth):
-        img[z] = template[z]
-    pl.semaphore_wait(barrier, ny + nz - 2)
-
     chunks = depth * EDGE // 8
     per = depth // chunks
 
@@ -191,47 +185,65 @@
     inner = (((EDGE, rows - 2 * EDGE, 0),), zmid, zrecv, 0)
     outer = (((0, EDGE, 0), (rows - EDGE, EDGE, EDGE)), zmid_edge, zrecv_edge, 1)
 
-    def z_copies(step, part):
+    def z_copies(step, part, halo=HALO, side=None):
         _, mid, received, which = part
-        return [copy(mid.at[step, pl.ds(0 if side else depth - HALO, HALO)],
-                     received.at[step, side], zs_send.at[step, side, which],
-                     zs_recv.at[step, side, which], at_z(1 - 2 * side)) for side in range(2)]
-
-    def put_edges(step, z, value):
-        ypad[z, pl.ds(8, rows), :] = value
-        ysend[step, 0, pl.ds(z * EDGE, EDGE), :] = value[rows - EDGE:, :]
-        ysend[step, 1, pl.ds(z * EDGE, EDGE), :] = value[:EDGE, :]
+        if side is None:
+            return [z_copies(step, part, halo, side) for side in range(2)]
+        return copy(mid.at[step, pl.ds((1 - side) * (depth - halo), halo)],
+                    received.at[step, side, pl.ds(0, halo)], zs_send.at[step, side, which],
+                    zs_recv.at[step, side, which], at_z(1 - 2 * side))
+
+    far_side = jnp.where(me_z < nz // 2, 1, 0)
+
+    def start_z(step, part, halo=HALO):
+        for side in (far_side, 1 - far_side):
+            z_copies(step, part, halo, side).start()
+
+    mine = pl.ds(2 * depth, 2 * depth)
+
+    def rim_copies():
+        return [copy(rim.at[mine], rim.at[pl.ds(side * 4 * depth, 2 * depth)],
+                     rs_send.at[side], rs_recv.at[side], at_z(1 - 2 * side)) for side in range(2)]
+
+    ahead = [copy(all_shifts.at[steps - 1, 2, depth - 1], zshift.at[0], zh_send.at[0],
+                  zh_recv.at[0], at_z(1)),
+             copy(all_shifts.at[steps - 1, 2, 0], zshift.at[1], zh_send.at[1], zh_recv.at[1],
+                  at_z(-1)),
+             copy(yshift_send.at[0], yshift.at[0], yh_send.at[0], yh_recv.at[0], at_y(1)),
+             copy(yshift_send.at[1], yshift.at[1], yh_send.at[1], yh_recv.at[1], at_y(-1))]
 
     def take_edges(step, z):
         ypad[z, pl.ds(8 - EDGE, EDGE), :] = yrecv[step, 0, pl.ds(z * EDGE, EDGE), :]
         ypad[z, pl.ds(8 + rows, EDGE), :] = yrecv[step, 1, pl.ds(z * EDGE, EDGE), :]
 
-    def advance(step, carry):
-        fetch_shifts(step).wait()
+    def pass_x(w, u, shift):
+        f = (w[0] * rolled(u, 1, 1) + w[1] * u + w[2] * rolled(u, -1, 1)
+             + w[3] * rolled(u, -2, 1))
+        return choose(shift, (rolled(f, 2, 1), rolled(f, 1, 1), f, rolled(f, -1, 1)))
+
+    def edges(step, source, start):
         w = cubic_weights(fractions[step, 0])
-
-        def pass_x(u, shift):
-            f = (w[0] * rolled(u, 1, 1) + w[1] * u + w[2] * rolled(u, -1, 1)
-                 + w[3] * rolled(u, -2, 1))
-            return choose(shift, (rolled(f, 2, 1), rolled(f, 1, 1), f, rolled(f, -1, 1)))
-
         first, last = pl.ds(0, EDGE), pl.ds(rows - EDGE, EDGE)
         for z in range(depth):
             value = pass_x(
-                jnp.concatenate([img[z, first, :], img[z, last, :]], axis=0),
+                w, jnp.concatenate([source[z, first, :], source[z, last, :]], axis=0),
                 jnp.concatenate([shifts[step, 0, z, first, :], shifts[step, 0, z, last, :]],
                                 axis=0))
             ypad[z, pl.ds(8, EDGE), :] = value[:EDGE, :]
             ypad[z, pl.ds(8 + rows - EDGE, EDGE), :] = value[EDGE:, :]
             ysend[step, 0, pl.ds(z * EDGE, EDGE), :] = value[EDGE:, :]
             ysend[step, 1, pl.ds(z * EDGE, EDGE), :] = value[:EDGE, :]
-            if z % per == per - 1:
+            if start and z % per == per - 1:
                 for c in y_copies(step, z // per):
                     c.start()
+
+    def rest(step, source, last):
+        halo = HALO + 1 if last else HALO
+        w_x = cubic_weights(fractions[step, 0])
         middle = pl.ds(EDGE, rows - 2 * EDGE)
         for z in range(depth):
             ypad[z, pl.ds(8 + EDGE, rows - 2 * EDGE), :] = pass_x(
-                img[z, middle, :], shifts[step, 0, z, middle, :])
+                w_x, source[z, middle, :], shifts[step, 0, z, middle, :])
         w = cubic_weights(fractions[step, 1])
 
         def pass_y(part, z):
@@ -246,75 +258,126 @@
 
         for z in range(depth):
             pass_y(inner, z)
-        for c in z_copies(step, inner):
-            c.start()
+        start_z(step, inner, halo)
         for z in range(depth):
             if z % per == 0:
                 for c in y_copies(step, z // per):
                     c.wait_recv()
             take_edges(step, z)
+            if last:
+                for m in range(7):
+                    rim_rows[m, pl.ds(2 * z, 1), :] = ypad[z, pl.ds(4 + m, 1), :]
+                    rim_rows[m, pl.ds(2 * z + 1, 1), :] = ypad[z, pl.ds(5 + rows + m, 1), :]
             pass_y(outer, z)
-        for c in z_copies(step, outer):
-            c.start()
+        if last:
+            for c in ahead:
+                c.wait_recv()
+            odd = lax.broadcasted_iota(jnp.int32, (2 * depth, width), 0) % 2 == 1
+
+            def rim_shift(at):
+                part = pl.ds(at, 2 * depth)
+                return jnp.where(odd, yshift[1, part, :], yshift[0, part, :])
+
+            rim[mine, :] = choose(rim_shift(2 * depth), [
+                w[0] * rim_rows[o] + w[1] * rim_rows[o + 1] + w[2] * rim_rows[o + 2]
+                + w[3] * rim_rows[o + 3] for o in range(4)])
+            for c in rim_copies():
+                c.start()
+        start_z(step, outer, halo)
         w_z = cubic_weights(fractions[step, 2])
 
         def pass_z(part):
             pieces, mid, received, _ = part
-            for c in z_copies(step, part):
+            for c in z_copies(step, part, halo):
                 c.wait_recv()
             size = sum(count for _, count, _ in pieces)
 
             def layer(k):
-                if k < HALO:
-                    return received[step, 0, k]
-                if k < HALO + depth:
-                    return mid[step, k - HALO]
-                return received[step, 1, k - HALO - depth]
-
-            for k in range(depth + 3):
-                zf[k, pl.ds(0, size), :] = (w_z[0] * layer(k) + w_z[1] * layer(k + 1)
-                                            + w_z[2] * layer(k + 2) + w_z[3] * layer(k + 3))
+                if k < 0:
+                    return received[step, 0, halo + k]
+                if k < depth:
+                    return mid[step, k]
+                return received[step, 1, k - depth]
+
+            low = 1 - halo
+            for k in range(low, depth + halo - 2):
+                zf[k - low, pl.ds(0, size), :] = (w_z[0] * layer(k - 1) + w_z[1] * layer(k)
+                                                  + w_z[2] * layer(k + 1) + w_z[3] * layer(k + 2))
+            for z in range(-1, depth + 1) if last else range(depth):
+                for start, count, at in pieces:
+                    part = pl.ds(start, count)
+                    options = [zf[z + o - 2 - low, pl.ds(at, count), :] for o in range(4)]
+                    if z < 0:
+                        beyond[0, part, :] = choose(zshift[0, part, :], options)
+                    elif z == depth:
+                        beyond[1, part, :] = choose(zshift[1, part, :], options)
+                    else:
+                        img[z, part, :] = choose(shifts[step, 2, z, part, :], options)
+
+        pass_z(inner)
+        if last:
+            for c in rim_copies():
+                c.wait_recv()
+            span = 2 * (depth + 3)
+            f = w_z[0] * rim[pl.ds(2 * depth - 6, span), :]
+            for n in range(1, 4):
+                f = f + w_z[n] * rim[pl.ds(2 * depth - 6 + 2 * n, span), :]
+            rim_f[...] = f
+            value = choose(rim_shift(0), [rim_f[pl.ds(2 * o, 2 * depth), :] for o in range(4)])
             for z in range(depth):
-                for start, count, at in pieces:
-                    img[z, pl.ds(start, count), :] = choose(
-                        shifts[step, 2, z, pl.ds(start, count), :],
-                        [zf[z + o, pl.ds(at, count), :] for o in range(4)])
-
-        pass_z(inner)
+                ypad[z, pl.ds(7, 1), :] = value[2 * z:2 * z + 1, :]
+                ypad[z, pl.ds(8 + rows, 1), :] = value[2 * z + 1:2 * z + 2, :]
         pass_z(outer)
         for chunk in range(chunks):
             for c in y_copies(step, chunk):
                 c.wait_send()
         for part in (inner, outer):
-            for c in z_copies(step, part):
+            for c in z_copies(step, part, halo):
                 c.wait_send()
+        if last:
+            for c in ahead + rim_copies():
+                c.wait_send()
+
+    def advance(step, carry):
+        rest(step, img, False)
+        edges(step + 1, img, True)
         return carry
 
-    lax.fori_loop(0, steps, advance, 0)
-
+    fetches[0].wait()
+    fetch_shifts(0).wait()
+    edges(0, template, False)
     for z in range(depth):
-        put_edges(steps, z, img[z])
-    copies = [c for chunk in range(chunks) for c in y_copies(steps, chunk)] + [
-        copy(img.at[depth - 1], grecv.at[0], gs_send.at[0], gs_recv.at[0], at_z(1)),
-        copy(img.at[0], grecv.at[1], gs_send.at[1], gs_recv.at[1], at_z(-1)),
-    ]
-    for c in copies:
+        img[z] = template[z]
+    for step in range(1, steps):
+        fetch_shifts(step).wait()
+    for place, kind in enumerate((2, 1)):
+        for z in range(depth):
+            for side, row in enumerate((rows - 1, 0)):
+                value = shifts[steps - 1, kind, z, pl.ds(row, 1), :]
+                for twin in range(2):
+                    yshift_send[side, pl.ds(2 * (place * depth + z) + twin, 1), :] = value
+    mixed[...] = jnp.zeros_like(mixed)
+    pl.semaphore_wait(barrier, ny + nz - 2)
+    for chunk in range(chunks):
+        for c in y_copies(0, chunk):
+            c.start()
+    for c in ahead:
         c.start()
+    lax.fori_loop(0, steps - 1, advance, 0)
+    rest(steps - 1, img, True)
+
     fetches[1].wait()
     for z in range(depth):
         u = img[z]
         deformed[z] = u
+        ypad[z, pl.ds(8, rows), :] = u
+        mismatch = u - target[z]
         forces[pl.ds(z * rows, rows), :] = (
-            (u - target[z]) * ((rolled(u, -1, 1) - rolled(u, 1, 1)) * 0.5))
-    for c in copies:
-        c.wait()
-    for z in range(depth):
-        take_edges(steps, z)
-        mismatch = img[z] - target[z]
+            mismatch * ((rolled(u, -1, 1) - rolled(u, 1, 1)) * 0.5))
         grad = (ypad[z, pl.ds(9, rows), :] - ypad[z, pl.ds(7, rows), :]) * 0.5
         forces[pl.ds((depth + z) * rows, rows), :] = mismatch * grad
-        above = img[z + 1] if z + 1 < depth else grecv[1]
-        below = img[z - 1] if z > 0 else grecv[0]
+        above = img[z + 1] if z + 1 < depth else beyond[1]
+        below = img[z - 1] if z > 0 else beyond[0]
         forces[pl.ds((2 * depth + z) * rows, rows), :] = mismatch * ((above - below) * 0.5)
 
     dc, rc, wc = depth // 2, rows // 2, width // 2
@@ -446,14 +509,20 @@
         vmem((depth, rows, width), f32),
         vmem((depth, rows + 16, width), f32),
         vmem((depth, rows + 8, width), f32),
-        vmem((steps + 1, 2, depth * EDGE, width), f32),
-        vmem((steps + 1, 2, depth * EDGE, width), f32),
+        vmem((steps, 2, depth * EDGE, width), f32),
+        vmem((steps, 2, depth * EDGE, width), f32),
         vmem((steps, depth, rows - 2 * EDGE, width), f32),
-        vmem((steps, 2, HALO, rows - 2 * EDGE, width), f32),
+        vmem((steps, 2, HALO + 1, rows - 2 * EDGE, width), f32),
         vmem((steps, depth, 2 * EDGE, width), f32),
-        vmem((steps, 2, HALO, 2 * EDGE, width), f32),
-        vmem((depth + 3, rows, width), f32),
+        vmem((steps, 2, HALO + 1, 2 * EDGE, width), f32),
+        vmem((depth + 5, rows, width), f32),
         vmem((2, rows, width), f32),
+        vmem((2, rows, width), shifts.dtype),
+        vmem((2, 4 * depth, width), shifts.dtype),
+        vmem((2, 4 * depth, width), shifts.dtype),
+        vmem((6 * depth, width), f32),
+        vmem((7, 2 * depth, width), f32),
+        vmem((2 * (depth + 3), width), f32),
         vmem((cz * rows, width), f32),
         vmem((cz * rows, width), f32),
         vmem((2 * cz, width), f32),
@@ -465,9 +534,9 @@
         vmem((3 * dc * rows, width), f32),
         vmem((cz * rows, width), bf16),
         vmem((cz * rows, width), bf16),
-        dma((steps + 1, 2, depth * EDGE // 8)), dma((steps + 1, 2, depth * EDGE // 8)),
+        dma((steps, 2, depth * EDGE // 8)), dma((steps, 2, depth * EDGE // 8)),
         dma((steps, 2, 2)), dma((steps, 2, 2)),
-        dma((2,)), dma((2,)),
+        dma((2,)), dma((2,)), dma((2,)), dma((2,)), dma((2,)), dma((2,)),
         dma((ny - 1,)), dma((ny - 1,)),
         dma((nz - 1,)), dma((nz - 1,)),
         dma((2,)), dma((2,)),

time: 52.7 us -> 50 us (0.949)
  Pallas kernels: 50.5 us -> 47.4 us
    pallas_call x1, Pallas kernels: 50.5 us -> 47.4 us  [on_device(): pl.pallas_call(functools.partial(kernel, ny, nz), out_shape=(vmem((3, dep...]
where the time goes in v3:
time: 50 us; the launch traced here: 49.5 us
  Pallas kernels  47.4 us (95%)
  local copies, waits for them, and re-layouts  1.4 us (3%)
  between operations  0.64 us (1%)
    pallas_call x1, Pallas kernels, on_device(): pl.pallas_call(functools.partial(kernel, ny, nz), out_shape=(vmem((3, dep...  47.4 us
    unnamed x2, local copies, waits for them, and re-layouts  1.4 us

profile of v3, /device:TPU:1, one launch (start us, length us, event | category | flops | bytes accessed | tf_op | source)
XLA Modules:
  0.0 49.5 jit_solution(14361112324166689890)
XLA Ops:
  0.6 47.4 %shard_map.158 = (f32[3,4,16,512]{3,2,1,0:T(8,128)S(1)}, f32[4,16,512]{2,1,0:T(8,128)S(1)}) custom-call(f32[4,3]{1,0:T(4,128)} %fractions.1, f32[4,16,512]{2,1,0:T(8,128)} %refs_0_.1, f32[4,16,512]{2,1,0:T(8,128)} %refs_1_.1, s32[4,3,4,16,512]{4,3,2,1,0:T(8,128)} %refs_2_.1, bf16[512,512]{1,0:T(8,128)(2,1)} %constant.22.clone.refs_3_, ...), custom_call_target="tpu_custom_call" | custom-call | tf_op jit(solution)/shard_map/pallas_call | solution.py:552
  48.0 0.7 %copy.19 = f32[3,4,16,512]{3,2,1,0:T(8,128)} copy(f32[3,4,16,512]{3,2,1,0:T(8,128)S(1)} %get-tuple-element.2) | data formatting | bytes 786432
  48.8 0.7 %copy.20 = f32[4,16,512]{2,1,0:T(8,128)} copy(f32[4,16,512]{2,1,0:T(8,128)S(1)} %get-tuple-element.3) | data formatting | bytes 262144

commit v4 on v3

--- a/solution.py
+++ b/solution.py
@@ -122,8 +122,16 @@
     return jnp.where(shift == -2, minus2, result)
 
 
-def kernel(ny, nz, fractions, *refs):
-    count = 14
+def kernel(ny, nz, *refs):
+    me_y, me_z = lax.axis_index("gy"), lax.axis_index("gz")
+    barrier = pltpu.get_barrier_semaphore()
+    for d in range(1, ny):
+        pl.semaphore_signal(barrier, inc=1, device_id=(lax.rem(me_y + d, ny), me_z),
+                            device_id_type=MESH)
+    for d in range(1, nz):
+        pl.semaphore_signal(barrier, inc=1, device_id=(me_y, lax.rem(me_z + d, nz)),
+                            device_id_type=MESH)
+    count = 15
     sources, (update, deformed), rest = refs[:count], refs[count:count + 2], refs[count + 2:]
     held, fetch_sems, shift_sems = rest[:count], rest[count], rest[count + 1]
     step_count = held[2].shape[0]
@@ -135,11 +143,12 @@
         return pltpu.make_async_copy(sources[2].at[step], held[2].at[step], shift_sems.at[step])
 
     fetches[0].start()
+    fetches[14].start()
     for step in range(step_count):
         fetch_shifts(step).start()
     for i in (1, 7, 8, 11, 3, 4, 5, 6, 13, 9, 10, 12):
         fetches[i].start()
-    body(ny, nz, fractions, fetches, fetch_shifts, sources[2], *held, update, deformed, *rest[count + 2:])
+    body(ny, nz, held[14], fetches, fetch_shifts, sources[2], *held[:14], update, deformed, *rest[count + 2:])
 
 
 def body(ny, nz, fractions, fetches, fetch_shifts, all_shifts, template, target, shifts, hart_hi, hart_lo,
@@ -163,12 +172,6 @@
         return pltpu.make_async_remote_copy(
             src_ref=src, dst_ref=dst, send_sem=send, recv_sem=recv, device_id=device,
             device_id_type=MESH)
-
-    barrier = pltpu.get_barrier_semaphore()
-    for d in range(1, ny):
-        pl.semaphore_signal(barrier, inc=1, device_id=at_y(d), device_id_type=MESH)
-    for d in range(1, nz):
-        pl.semaphore_signal(barrier, inc=1, device_id=at_z(d), device_id_type=MESH)
 
     def rolled(value, by, axis):
         return pltpu.roll(value, by % value.shape[axis], axis)
@@ -343,6 +346,7 @@
         edges(step + 1, img, True)
         return carry
 
+    fetches[14].wait()
     fetches[0].wait()
     fetch_shifts(0).wait()
     edges(0, template, False)
@@ -357,7 +361,7 @@
                 for twin in range(2):
                     yshift_send[side, pl.ds(2 * (place * depth + z) + twin, 1), :] = value
     mixed[...] = jnp.zeros_like(mixed)
-    pl.semaphore_wait(barrier, ny + nz - 2)
+    pl.semaphore_wait(pltpu.get_barrier_semaphore(), ny + nz - 2)
     for chunk in range(chunks):
         for c in y_copies(0, chunk):
             c.start()
@@ -413,11 +417,23 @@
         msend[pl.ds(cz + k, 1), :] = jnp.sum(g * tables[1], axis=0, keepdims=True)
     moments = [copy(msend, mrecv.at[d - 1], ms_send.at[d - 1], ms_recv.at[d - 1], at_y(d))
                for d in range(1, ny)]
-    for c in moments:
-        c.start()
+    for d in sorted(range(1, ny), key=lambda d: -min(d, ny - d)):
+        moments[d - 1].start()
+    levels = (tables.shape[0] - 5) // 2
+    for k in range(cz):
+        g = ghat[pl.ds(k * rows, rows), :]
+        down, up = g, g
+        for level in range(levels):
+            down = down + tables[5 + level] * rolled(down, 1 << level, 0)
+            up = up + tables[5 + levels + level] * rolled(up, -(1 << level), 0)
+        ghat[pl.ds(k * rows, rows), :] = tables[4] * (down + (up - g))
     fetches[13].wait()
     for d in range(1, nz):
         copy(coarse.at[0], coarse.at[d], cs_send.at[d - 1], cs_recv.at[d - 1], at_z(-d)).wait()
+    sides = [[copy(parts.at[1 + side, pl.ds(c * dc * rc, dc * rc)],
+                   arrived.at[side, pl.ds(c * dc * rc, dc * rc)], hs_send.at[side, c],
+                   hs_recv.at[side, c], at_y(2 * side - 1)) for side in range(2)]
+             for c in range(3)]
     total, far = nz * dc, far_layers(nz * dc)
     lanes = min(wc, 128)
     for c in range(3):
@@ -454,10 +470,8 @@
                             add(2, tap * at[3])
                 for side in range(3):
                     parts[side, pl.ds((c * dc + a) * rc, rc), across] = sums[side]
-    sides = [copy(parts.at[1], arrived.at[0], hs_send.at[0], hs_recv.at[0], at_y(-1)),
-             copy(parts.at[2], arrived.at[1], hs_send.at[1], hs_recv.at[1], at_y(1))]
-    for c in sides:
-        c.start()
+        for side in sides[c]:
+            side.start()
     for c in moments:
         c.wait()
     fetches[6].wait()
@@ -466,14 +480,8 @@
     for m in range(1, ny):
         from_left = from_left + hops[pl.ds(m - 1, 1), :] * mrecv[m - 1, pl.ds(0, cz), :]
         from_right = from_right + hops[pl.ds(m - 1, 1), :] * mrecv[ny - m - 1, pl.ds(cz, cz), :]
-    levels = (tables.shape[0] - 5) // 2
     for k in range(cz):
-        g = ghat[pl.ds(k * rows, rows), :]
-        down, up = g, g
-        for level in range(levels):
-            down = down + tables[5 + level] * rolled(down, 1 << level, 0)
-            up = up + tables[5 + levels + level] * rolled(up, -(1 << level), 0)
-        s = (tables[4] * (down + (up - g)) + tables[2] * from_left[k:k + 1, :]
+        s = (ghat[pl.ds(k * rows, rows), :] + tables[2] * from_left[k:k + 1, :]
              + tables[3] * from_right[k:k + 1, :])
         high, low = split(s)
         fhi[pl.ds(k * rows, rows), :] = high
@@ -482,8 +490,9 @@
 
     for i in (9, 10, 12):
         fetches[i].wait()
-    for c in sides:
-        c.wait()
+    for pair in sides:
+        for c in pair:
+            c.wait()
     high, low = split(parts[0] + (arrived[0] + arrived[1]))
     tall = f32dot(spread_y[...], high) + f32dot(spread_y[...], low)
     high, low = split(tall)
@@ -539,25 +548,24 @@
         dma((2,)), dma((2,)), dma((2,)), dma((2,)), dma((2,)), dma((2,)),
         dma((ny - 1,)), dma((ny - 1,)),
         dma((nz - 1,)), dma((nz - 1,)),
-        dma((2,)), dma((2,)),
+        dma((2, 3)), dma((2, 3)),
     ]
     spec = pl.BlockSpec(memory_space=pltpu.VMEM)
-    smem = pl.BlockSpec(memory_space=pltpu.SMEM)
     hbm = pl.BlockSpec(memory_space=pltpu.HBM)
     operands = [template, target, shifts, jnp.asarray(hart_hi), jnp.asarray(hart_lo),
                 *map(jnp.asarray, (tables, hops, fold_hi, fold_lo, spread_hi, spread_lo, pair_y,
-                                   spread_y, taps))]
-    held = [vmem(x.shape, x.dtype) for x in operands]
+                                   spread_y, taps)), fractions]
+    held = [vmem(x.shape, x.dtype) for x in operands[:-1]] + [pltpu.SMEM(fractions.shape, f32)]
     scratch = held + [dma((len(operands),)), dma((steps,))] + scratch
     return tuple(pl.pallas_call(
         functools.partial(kernel, ny, nz),
         out_shape=(vmem((3, depth, rows, width), f32), vmem((depth, rows, width), f32)),
-        in_specs=[smem] + [hbm] * len(operands),
+        in_specs=[hbm] * len(operands),
         out_specs=(spec, spec),
         scratch_shapes=scratch,
         compiler_params=pltpu.CompilerParams(
             collective_id=0, has_side_effects=True),
-    )(fractions, *operands))
+    )(*operands))
 
 
 def solution(mesh):

time: 50 us -> 49.3 us (0.986)
  Pallas kernels: 47.4 us -> 46.7 us
    pallas_call x1, Pallas kernels: 47.4 us -> 46.7 us  [on_device(): pl.pallas_call(functools.partial(kernel, ny, nz), out_shape=(vmem((3, dep...]
where the time goes in v4:
time: 49.3 us; the launch traced here: 48.8 us
  Pallas kernels  46.7 us (95%)
  local copies, waits for them, and re-layouts  1.4 us (3%)
  between operations  0.64 us (1%)
    pallas_call x1, Pallas kernels, on_device(): pl.pallas_call(functools.partial(kernel, ny, nz), out_shape=(vmem((3, dep...  46.7 us
    unnamed x2, local copies, waits for them, and re-layouts  1.4 us

profile of v4, /device:TPU:1, one launch (start us, length us, event | category | flops | bytes accessed | tf_op | source)
XLA Modules:
  0.0 48.8 jit_solution(3167479657655783835)
XLA Ops:
  0.6 46.7 %shard_map.158 = (f32[3,4,16,512]{3,2,1,0:T(8,128)S(1)}, f32[4,16,512]{2,1,0:T(8,128)S(1)}) custom-call(f32[4,16,512]{2,1,0:T(8,128)} %refs_0_.1, f32[4,16,512]{2,1,0:T(8,128)} %refs_1_.1, s32[4,3,4,16,512]{4,3,2,1,0:T(8,128)} %refs_2_.1, bf16[512,512]{1,0:T(8,128)(2,1)} %constant.22.clone.refs_3_, bf16[512,512]{1,0:T(8,128)(2,1)} %constant.23.clone.refs_4_, ...), custom_call_target="tpu_custom_call" | custom-call | tf_op jit(solution)/shard_map/pallas_call | solution.py:560
  47.4 0.7 %copy.19 = f32[3,4,16,512]{3,2,1,0:T(8,128)} copy(f32[3,4,16,512]{3,2,1,0:T(8,128)S(1)} %get-tuple-element.2) | data formatting | bytes 786432
  48.1 0.7 %copy.20 = f32[4,16,512]{2,1,0:T(8,128)} copy(f32[4,16,512]{2,1,0:T(8,128)S(1)} %get-tuple-element.3) | data formatting | bytes 262144

commit v5 on v4

--- a/solution.py
+++ b/solution.py
@@ -131,7 +131,7 @@
     for d in range(1, nz):
         pl.semaphore_signal(barrier, inc=1, device_id=(me_y, lax.rem(me_z + d, nz)),
                             device_id_type=MESH)
-    count = 15
+    count = 13
     sources, (update, deformed), rest = refs[:count], refs[count:count + 2], refs[count + 2:]
     held, fetch_sems, shift_sems = rest[:count], rest[count], rest[count + 1]
     step_count = held[2].shape[0]
@@ -143,18 +143,18 @@
         return pltpu.make_async_copy(sources[2].at[step], held[2].at[step], shift_sems.at[step])
 
     fetches[0].start()
-    fetches[14].start()
+    fetches[12].start()
     for step in range(step_count):
         fetch_shifts(step).start()
-    for i in (1, 7, 8, 11, 3, 4, 5, 6, 13, 9, 10, 12):
+    for i in (1, 7, 8, 3, 4, 5, 6, 11, 9, 10):
         fetches[i].start()
-    body(ny, nz, held[14], fetches, fetch_shifts, sources[2], *held[:14], update, deformed, *rest[count + 2:])
+    body(ny, nz, held[12], fetches, fetch_shifts, sources[2], *held[:12], update, deformed, *rest[count + 2:])
 
 
 def body(ny, nz, fractions, fetches, fetch_shifts, all_shifts, template, target, shifts, hart_hi, hart_lo,
-         tables, hops, fold_hi, fold_lo, spread_hi, spread_lo, pair_y, spread_y, taps,
+         tables, hops, fold_hi, fold_lo, spread_hi, spread_lo, taps,
          update, deformed, img, ypad, yf, ysend, yrecv, zmid, zrecv, zmid_edge, zrecv_edge,
-           zf, beyond, zshift, yshift_send, yshift, rim, rim_rows, rim_f, forces, ghat, msend, mrecv, coarse, parts, arrived, mixed,
+           zf, beyond, zshift, yshift_send, yshift, rim, rim_rows, rim_f, forces, ghat, msend, mrecv, coarse, parts, arrived, mixed, tall,
            zsum, fhi, flo, ys_send, ys_recv, zs_send, zs_recv, rs_send, rs_recv, zh_send, zh_recv, yh_send, yh_recv, ms_send, ms_recv,
            cs_send, cs_recv, hs_send, hs_recv):
     depth, rows, width = template.shape
@@ -346,7 +346,7 @@
         edges(step + 1, img, True)
         return carry
 
-    fetches[14].wait()
+    fetches[12].wait()
     fetches[0].wait()
     fetch_shifts(0).wait()
     edges(0, template, False)
@@ -385,27 +385,34 @@
         forces[pl.ds((2 * depth + z) * rows, rows), :] = mismatch * ((above - below) * 0.5)
 
     dc, rc, wc = depth // 2, rows // 2, width // 2
+    lanes = min(wc, 128)
     for c in range(3):
         for z in range(dc):
             base = (c * depth + 2 * z) * rows
             zsum[pl.ds((c * dc + z) * rows, rows), :] = (
                 forces[pl.ds(base, rows), :] + forces[pl.ds(base + rows, rows), :])
-    for i in (7, 8, 11):
+    for i in (7, 8):
         fetches[i].wait()
-    f32dot = functools.partial(jnp.dot, preferred_element_type=jnp.float32)
     high, low = split(zsum[...])
-    high, low = split(dot3(high, low, fold_hi[...], fold_lo[...]))
-    coarse[0] = f32dot(pair_y[...], high) + f32dot(pair_y[...], low)
-    gathers = []
+    folded = dot3(high, low, fold_hi[...], fold_lo[...])
+    pairs = 3 * dc * rc
+    for h in range(wc // lanes):
+        across = pl.ds(h * lanes, lanes)
+        tall[h] = folded[:, h * lanes:(h + 1) * lanes]
+        coarse[0, :, across] = (tall[h, pl.ds(0, pairs, stride=2), :]
+                                + tall[h, pl.ds(1, pairs, stride=2), :])
+    per_c = dc * rc
+
+    def gather(d, c, device):
+        return copy(coarse.at[0, pl.ds(c * per_c, per_c)], coarse.at[d, pl.ds(c * per_c, per_c)],
+                    cs_send.at[d - 1, c], cs_recv.at[d - 1, c], device)
+
     for k in range(nz - 1):
         away = jnp.where(me_z < nz // 2, nz - 1 - k, k)
         away = away + jnp.where(me_z < nz // 2, -(away <= me_z).astype(jnp.int32),
                                 (away >= me_z).astype(jnp.int32))
-        slot = lax.rem(me_z - away + nz, nz)
-        gathers.append(copy(coarse.at[0], coarse.at[slot], cs_send.at[slot - 1],
-                            cs_recv.at[slot - 1], (me_y, away)))
-    for c in gathers:
-        c.start()
+        for c in range(3):
+            gather(lax.rem(me_z - away + nz, nz), c, (me_y, away)).start()
 
     for i in (3, 4, 5):
         fetches[i].wait()
@@ -415,10 +422,20 @@
         g = ghat[pl.ds(k * rows, rows), :]
         msend[pl.ds(k, 1), :] = jnp.sum(g * tables[0], axis=0, keepdims=True)
         msend[pl.ds(cz + k, 1), :] = jnp.sum(g * tables[1], axis=0, keepdims=True)
-    moments = [copy(msend, mrecv.at[d - 1], ms_send.at[d - 1], ms_recv.at[d - 1], at_y(d))
-               for d in range(1, ny)]
-    for d in sorted(range(1, ny), key=lambda d: -min(d, ny - d)):
-        moments[d - 1].start()
+    odd_core = lax.rem(me_y, 2)
+    partner = (me_y + 1 - 2 * odd_core, me_z)
+
+    def moment(d):
+        return copy(msend, mrecv.at[d - 1], ms_send.at[d - 1], ms_recv.at[d - 1], at_y(d))
+
+    def to_partner(d):
+        slot = lax.rem(d + ny - 2 * odd_core, ny)
+        return copy(msend if d == 0 else mrecv.at[d - 1], mrecv.at[slot], ms_send.at[d],
+                    ms_recv.at[slot], partner)
+
+    for d in range(2, ny, 2):
+        moment(d).start()
+    to_partner(0).start()
     levels = (tables.shape[0] - 5) // 2
     for k in range(cz):
         g = ghat[pl.ds(k * rows, rows), :]
@@ -427,16 +444,15 @@
             down = down + tables[5 + level] * rolled(down, 1 << level, 0)
             up = up + tables[5 + levels + level] * rolled(up, -(1 << level), 0)
         ghat[pl.ds(k * rows, rows), :] = tables[4] * (down + (up - g))
-    fetches[13].wait()
-    for d in range(1, nz):
-        copy(coarse.at[0], coarse.at[d], cs_send.at[d - 1], cs_recv.at[d - 1], at_z(-d)).wait()
+    fetches[11].wait()
     sides = [[copy(parts.at[1 + side, pl.ds(c * dc * rc, dc * rc)],
                    arrived.at[side, pl.ds(c * dc * rc, dc * rc)], hs_send.at[side, c],
                    hs_recv.at[side, c], at_y(2 * side - 1)) for side in range(2)]
              for c in range(3)]
     total, far = nz * dc, far_layers(nz * dc)
-    lanes = min(wc, 128)
     for c in range(3):
+        for d in range(1, nz):
+            gather(d, c, at_z(-d)).wait()
         for h in range(wc // lanes):
             across = pl.ds(h * lanes, lanes)
 
@@ -472,8 +488,16 @@
                     parts[side, pl.ds((c * dc + a) * rc, rc), across] = sums[side]
         for side in sides[c]:
             side.start()
-    for c in moments:
-        c.wait()
+        if c == 0:
+            for d in range(2, ny, 2):
+                moment(d).wait_recv()
+                to_partner(d).start()
+    for d in range(1, ny, 2):
+        moment(d).wait_recv()
+    for d in range(2, ny, 2):
+        moment(d).wait_send()
+    for d in range(0, ny, 2):
+        to_partner(d).wait_send()
     fetches[6].wait()
     from_left = hops[pl.ds(ny - 1, 1), :] * msend[pl.ds(0, cz), :]
     from_right = hops[pl.ds(ny - 1, 1), :] * msend[pl.ds(cz, cz), :]
@@ -488,19 +512,24 @@
         flo[pl.ds(k * rows, rows), :] = low
     ghat[...] = dot3(fhi[...], flo[...], hart_hi[...], hart_lo[...])
 
-    for i in (9, 10, 12):
+    for i in (9, 10):
         fetches[i].wait()
     for pair in sides:
         for c in pair:
             c.wait()
     high, low = split(parts[0] + (arrived[0] + arrived[1]))
-    tall = f32dot(spread_y[...], high) + f32dot(spread_y[...], low)
-    high, low = split(tall)
-    zsum[...] = dot3(high, low, spread_hi[...], spread_lo[...])
+    short = dot3(high, low, spread_hi[...], spread_lo[...])
+    for h in range(width // lanes):
+        value = short[:, h * lanes:(h + 1) * lanes]
+        for twin in range(2):
+            tall[h, pl.ds(twin, pairs, stride=2), :] = value
     for c in range(3):
         for z in range(depth):
-            fine = zsum[pl.ds((c * dc + z // 2) * rows, rows), :]
-            update[c, z] = -(ghat[pl.ds((c * depth + z) * rows, rows), :] + fine)
+            for h in range(width // lanes):
+                across = pl.ds(h * lanes, lanes)
+                fine = tall[h, pl.ds((c * dc + z // 2) * rows, rows), :]
+                update[c, z, :, across] = -(ghat[pl.ds((c * depth + z) * rows, rows), across]
+                                            + fine)
 
 
 def on_device(template, target, shifts, fractions, *, ny, nz):
@@ -510,8 +539,6 @@
     cz = 3 * depth
     hart_hi, hart_lo, tables, hops = make_tables(rows, width, ny)
     fold_hi, fold_lo, spread_hi, spread_lo, taps = make_coarse(width, nz * dc, ny * rc)
-    pair_y = np.kron(np.eye(3 * dc * rc), np.ones((1, 2))).astype(jnp.bfloat16)
-    spread_y = np.ascontiguousarray(pair_y.T)
     f32, bf16 = jnp.float32, jnp.bfloat16
     vmem, dma = pltpu.VMEM, pltpu.SemaphoreType.DMA
     scratch = [
@@ -540,6 +567,7 @@
         vmem((3, 3 * dc * rc, wc), f32),
         vmem((2, 3 * dc * rc, wc), f32),
         vmem((-(-wc // 128), dc * far_layers(nz * dc), 3 * rc, min(wc, 128)), f32),
+        vmem((width // min(wc, 128), 3 * dc * rows, min(wc, 128)), f32),
         vmem((3 * dc * rows, width), f32),
         vmem((cz * rows, width), bf16),
         vmem((cz * rows, width), bf16),
@@ -547,14 +575,14 @@
         dma((steps, 2, 2)), dma((steps, 2, 2)),
         dma((2,)), dma((2,)), dma((2,)), dma((2,)), dma((2,)), dma((2,)),
         dma((ny - 1,)), dma((ny - 1,)),
-        dma((nz - 1,)), dma((nz - 1,)),
+        dma((nz - 1, 3)), dma((nz - 1, 3)),
         dma((2, 3)), dma((2, 3)),
     ]
     spec = pl.BlockSpec(memory_space=pltpu.VMEM)
     hbm = pl.BlockSpec(memory_space=pltpu.HBM)
     operands = [template, target, shifts, jnp.asarray(hart_hi), jnp.asarray(hart_lo),
-                *map(jnp.asarray, (tables, hops, fold_hi, fold_lo, spread_hi, spread_lo, pair_y,
-                                   spread_y, taps)), fractions]
+                *map(jnp.asarray, (tables, hops, fold_hi, fold_lo, spread_hi, spread_lo, taps)),
+                fractions]
     held = [vmem(x.shape, x.dtype) for x in operands[:-1]] + [pltpu.SMEM(fractions.shape, f32)]
     scratch = held + [dma((len(operands),)), dma((steps,))] + scratch
     return tuple(pl.pallas_call(

time: 49.3 us -> 48.7 us (0.988)
  no operation moved by 1% of the time
where the time goes in v5:
time: 48.7 us; the launch traced here: 48.6 us
  Pallas kernels  46.5 us (95%)
  local copies, waits for them, and re-layouts  1.4 us (3%)
  between operations  0.64 us (1%)
    pallas_call x1, Pallas kernels, on_device(): pl.pallas_call(functools.partial(kernel, ny, nz), out_shape=(vmem((3, dep...  46.5 us
    unnamed x2, local copies, waits for them, and re-layouts  1.4 us

profile of v5, /device:TPU:1, one launch (start us, length us, event | category | flops | bytes accessed | tf_op | source)
XLA Modules:
  0.0 48.6 jit_solution(12856805806848855322)
XLA Ops:
  0.6 46.5 %shard_map.140 = (f32[3,4,16,512]{3,2,1,0:T(8,128)S(1)}, f32[4,16,512]{2,1,0:T(8,128)S(1)}) custom-call(f32[4,16,512]{2,1,0:T(8,128)} %refs_0_.1, f32[4,16,512]{2,1,0:T(8,128)} %refs_1_.1, s32[4,3,4,16,512]{4,3,2,1,0:T(8,128)} %refs_2_.1, bf16[512,512]{1,0:T(8,128)(2,1)} %constant.18.clone.refs_3_, bf16[512,512]{1,0:T(8,128)(2,1)} %constant.19.clone.refs_4_, ...), custom_call_target="tpu_custom_call" | custom-call | tf_op jit(solution)/shard_map/pallas_call | solution.py:588
  47.2 0.7 %copy.17 = f32[3,4,16,512]{3,2,1,0:T(8,128)} copy(f32[3,4,16,512]{3,2,1,0:T(8,128)S(1)} %get-tuple-element.2) | data formatting | bytes 786432
  47.9 0.7 %copy.18 = f32[4,16,512]{2,1,0:T(8,128)} copy(f32[4,16,512]{2,1,0:T(8,128)S(1)} %get-tuple-element.3) | data formatting | bytes 262144

commit v6 on v5

--- a/solution.py
+++ b/solution.py
@@ -220,9 +220,9 @@
         ypad[z, pl.ds(8 + rows, EDGE), :] = yrecv[step, 1, pl.ds(z * EDGE, EDGE), :]
 
     def pass_x(w, u, shift):
-        f = (w[0] * rolled(u, 1, 1) + w[1] * u + w[2] * rolled(u, -1, 1)
-             + w[3] * rolled(u, -2, 1))
-        return choose(shift, (rolled(f, 2, 1), rolled(f, 1, 1), f, rolled(f, -1, 1)))
+        at = [rolled(u, 3 - m, 1) if m != 3 else u for m in range(7)]
+        picked = [choose(shift, at[n:n + 4]) for n in range(4)]
+        return w[0] * picked[0] + w[1] * picked[1] + w[2] * picked[2] + w[3] * picked[3]
 
     def edges(step, source, start):
         w = cubic_weights(fractions[step, 0])

time: 48.7 us -> 48.5 us (level)
  no operation moved by 1% of the time
where the time goes in v6:
time: 48.5 us; the launch traced here: 48.3 us
  Pallas kernels  46.3 us (95%)
  local copies, waits for them, and re-layouts  1.4 us (3%)
  between operations  0.64 us (1%)
    pallas_call x1, Pallas kernels, on_device(): pl.pallas_call(functools.partial(kernel, ny, nz), out_shape=(vmem((3, dep...  46.3 us
    unnamed x2, local copies, waits for them, and re-layouts  1.4 us

profile of v6, /device:TPU:1, one launch (start us, length us, event | category | flops | bytes accessed | tf_op | source)
XLA Modules:
  0.0 48.3 jit_solution(7454757054137023289)
XLA Ops:
  0.6 46.3 %shard_map.140 = (f32[3,4,16,512]{3,2,1,0:T(8,128)S(1)}, f32[4,16,512]{2,1,0:T(8,128)S(1)}) custom-call(f32[4,16,512]{2,1,0:T(8,128)} %refs_0_.1, f32[4,16,512]{2,1,0:T(8,128)} %refs_1_.1, s32[4,3,4,16,512]{4,3,2,1,0:T(8,128)} %refs_2_.1, bf16[512,512]{1,0:T(8,128)(2,1)} %constant.18.clone.refs_3_, bf16[512,512]{1,0:T(8,128)(2,1)} %constant.19.clone.refs_4_, ...), custom_call_target="tpu_custom_call" | custom-call | tf_op jit(solution)/shard_map/pallas_call | solution.py:588
  46.9 0.7 %copy.17 = f32[3,4,16,512]{3,2,1,0:T(8,128)} copy(f32[3,4,16,512]{3,2,1,0:T(8,128)S(1)} %get-tuple-element.2) | data formatting | bytes 786432
  47.7 0.7 %copy.18 = f32[4,16,512]{2,1,0:T(8,128)} copy(f32[4,16,512]{2,1,0:T(8,128)S(1)} %get-tuple-element.3) | data formatting | bytes 262144
